TPU v7x, 256 devices: a whole 4x4x8 slice. The times are simulated.
256 devices in a mesh: seq: 16 (over x, y_hi, core), fsdp: 16 (over z, y_lo).
Axes of the slice: x: 4, y: 4 (y_hi: 2, y_lo: 2; y = y_hi * 2 + y_lo), z: 8, core: 2. Of those that a mesh axis runs over, the one named last changes fastest.
Arguments:
- hidden: bfloat16 [32768, 8192], P(('seq', 'fsdp')), may hold values from -24 to 24
- kv_blocks: bfloat16 [8192, 1024], P('fsdp'), may hold values from -0.0625 to 0.0625
- kv_scale: float32 [64, 8], P('fsdp'), may hold values from 0.5 to 2
- queries: bfloat16 [32768, 4096], P(('seq', 'fsdp')), may hold values from -24 to 24
- grad_out: bfloat16 [32768, 4096], P(('seq', 'fsdp')), may hold values from -6 to 6
Outputs:
- attn_out: bfloat16 [32768, 4096], P(('seq', 'fsdp'))
- grad_queries: bfloat16 [32768, 4096], P(('seq', 'fsdp'))
- grad_hidden: bfloat16 [32768, 8192], P(('seq', 'fsdp'))
- weight_grad: float32 [8192, 1024], P('fsdp')
All inputs are finite; a program needn't handle non-finite values.
Results may differ from a plain program's by a relative error of at most 0.0075.
The roundings to bfloat16 on the way count: a program that leaves them out, or rounds other values in their place, can miss the bound.
Values may be sent and summed in bfloat16 or wider, within the bound.
No kernel may reach another device: no remote copies, remote signals or barrier semaphores. Data moves between devices by JAX's collectives and lax.ppermute only.
A program may use at most 128 MiB of HBM per device.

v0:
```python
import jax
import jax.numpy as jnp
from jax import lax
from jax.sharding import Mesh
from jax.sharding import PartitionSpec as P

HEADS = 32
KV_HEADS = 4
HEAD = 128
QB = 128
FSDP = ("fsdp_0", "fsdp_1")
SEQ_FSDP = ("seq", "fsdp_0", "fsdp_1")
NEG = -1e30


def gather_axes(value, axes, dim):
    if not axes:
        return value
    nearer = lax.all_gather(value, axes[-1], axis=dim, tiled=True)
    return gather_axes(nearer, axes[:-1], dim)


def shifted(block, axis, distance):
    devices = range(lax.axis_size(axis))
    route = [(i - distance, i) for i in devices if i - distance in devices]
    return lax.ppermute(block, axis, route)


def dequantize(blocks, scale):
    rows, cols = blocks.shape
    grid = blocks.astype(jnp.float32).reshape(scale.shape[0], QB, scale.shape[1], QB)
    return (grid * scale[:, None, :, None]).reshape(rows, cols).astype(jnp.bfloat16)


def attend_group(operands, allowed):
    qgrp, kgrp, vgrp, ggrp = operands
    factor = 1.0 / float(HEAD) ** 0.5
    scores = jnp.einsum("rhd,kd->rhk", qgrp, kgrp, preferred_element_type=jnp.float32) * factor
    scores = jnp.where(allowed[:, None, :], scores, NEG)
    top = jnp.max(scores, axis=-1, keepdims=True)
    expd = jnp.exp(scores - top)
    probs = expd / jnp.sum(expd, axis=-1, keepdims=True)
    probs_b = probs.astype(jnp.bfloat16)
    output = jnp.einsum("rhk,kd->rhd", probs_b, vgrp, preferred_element_type=jnp.float32).astype(
        jnp.bfloat16
    )
    dprobs = jnp.einsum("rhd,kd->rhk", ggrp, vgrp, preferred_element_type=jnp.float32)
    delta = jnp.sum(probs * dprobs, axis=-1, keepdims=True)
    dscores = (probs * (dprobs - delta) * factor).astype(jnp.bfloat16)
    gradq = jnp.einsum("rhk,kd->rhd", dscores, kgrp, preferred_element_type=jnp.float32).astype(
        jnp.bfloat16
    )
    gradk = jnp.einsum("rhk,rhd->kd", dscores, qgrp, preferred_element_type=jnp.float32)
    gradv = jnp.einsum("rhk,rhd->kd", probs_b, ggrp, preferred_element_type=jnp.float32)
    return (output, gradq, gradk, gradv)


def attend(queries, window, grad_out, allowed):
    rows = queries.shape[0]
    count = window.shape[0]
    group = HEADS // KV_HEADS
    kvw = KV_HEADS * HEAD
    qgrp = queries.reshape(rows, KV_HEADS, group, HEAD).transpose(1, 0, 2, 3)
    ggrp = grad_out.reshape(rows, KV_HEADS, group, HEAD).transpose(1, 0, 2, 3)
    kgrp = window[:, :kvw].reshape(count, KV_HEADS, HEAD).transpose(1, 0, 2)
    vgrp = window[:, kvw:].reshape(count, KV_HEADS, HEAD).transpose(1, 0, 2)
    output, gradq, gradk, gradv = lax.map(
        lambda ops: attend_group(ops, allowed), (qgrp, kgrp, vgrp, ggrp)
    )
    output = output.transpose(1, 0, 2, 3).reshape(rows, HEADS * HEAD)
    gradq = gradq.transpose(1, 0, 2, 3).reshape(rows, HEADS * HEAD)
    gradk = gradk.transpose(1, 0, 2).reshape(count, kvw)
    gradv = gradv.transpose(1, 0, 2).reshape(count, kvw)
    return (output, gradq, jnp.concatenate([gradk, gradv], axis=1))


def body(hidden, kv_blocks, kv_scale, queries, grad_out):
    tok = hidden.shape[0]
    groups = lax.axis_size(FSDP)
    reach = groups // 2
    place = lax.axis_index(FSDP)
    linear = lax.axis_index("seq") * groups + place
    weights = dequantize(kv_blocks, kv_scale)
    columns = lax.all_to_all(hidden, FSDP, split_axis=1, concat_axis=0, tiled=True)
    whole = gather_axes(weights, FSDP, 0)
    kv = jnp.dot(hidden, whole, preferred_element_type=jnp.float32).astype(jnp.bfloat16)
    pieces = []
    for offset in range(reach, 0, -1):
        pieces.append(shifted(kv, SEQ_FSDP, offset))
    window = jnp.concatenate(pieces + [kv], axis=0)
    base = linear * tok
    qpos = base + jnp.arange(tok, dtype=jnp.int32)
    kpos = base - reach * tok + jnp.arange((reach + 1) * tok, dtype=jnp.int32)
    span = reach * tok
    allowed = (
        (qpos[:, None] - kpos[None, :] < span)
        & (kpos[None, :] <= qpos[:, None])
        & (kpos[None, :] >= 0)
    )
    attn_out, grad_queries, dwin = attend(queries, window, grad_out, allowed)
    total = dwin[reach * tok :]
    inside = total
    for offset in range(1, reach + 1):
        piece = dwin[(reach - offset) * tok : (reach - offset + 1) * tok]
        returned = shifted(piece, SEQ_FSDP, -offset)
        total = total + returned
        inside = inside + jnp.where(place + offset < groups, returned, jnp.zeros_like(returned))
    all_grad = total.astype(jnp.bfloat16)
    seg_grad = inside.astype(jnp.bfloat16)
    grad_hidden = lax.dot_general(
        seg_grad, whole, (((1,), (1,)), ((), ())), preferred_element_type=jnp.float32
    ).astype(jnp.bfloat16)
    shard_grad = lax.dot_general(
        columns,
        lax.all_gather(all_grad, FSDP, axis=0, tiled=True),
        (((0,), (0,)), ((), ())),
        preferred_element_type=jnp.float32,
    )
    weight_grad = lax.psum(shard_grad, "seq")
    return (attn_out, grad_queries, grad_hidden, weight_grad)


def solution(mesh):
    finer = Mesh(mesh.devices.reshape(mesh.shape["seq"], 8, 2), ("seq", "fsdp_0", "fsdp_1"))
    placed = (P(SEQ_FSDP, None), P(FSDP, None), P(FSDP, None), P(SEQ_FSDP, None), P(SEQ_FSDP, None))
    return jax.shard_map(
        body,
        mesh=finer,
        in_specs=placed,
        out_specs=(P(SEQ_FSDP, None), P(SEQ_FSDP, None), P(SEQ_FSDP, None), P(FSDP, None)),
        check_vma=False,
    )
```

profile of v0, /device:TPU:1, one launch (start us, length us, event | category | flops | bytes accessed | tf_op | source)
XLA Modules:
  0.0 1012.2 jit_solution(2476808071577137936)
XLA Ops:
  10.0 42.4 %all-gather.4.cloned.1.call-done = bf16[1024,1024]{1,0:T(8,128)(2,1)} async-done(((bf16[512,1024]{1,0:T(8,128)(2,1)}), bf16[1024,1024]{1,0:T(8,128)(2,1)}) %all-gather.4.cloned.1.call-update) | async-done | bytes 2097168 | tf_op jit(solution)/shard_map/all_gather | solution.py:19
  52.5 175.5 %all-gather.6.cloned.1.call-done = bf16[8192,1024]{1,0:T(8,128)(2,1)} async-done(((bf16[1024,1024]{1,0:T(8,128)(2,1)}), bf16[8192,1024]{1,0:T(8,128)(2,1)}) %all-gather.6.cloned.1.call-update) | async-done | bytes 16777232 | tf_op jit(solution)/shard_map/all_gather | solution.py:19
  271.7 18.8 %collective-permute-done.2 = bf16[128,1024]{1,0:T(8,128)(2,1)S(1)} collective-permute-done((bf16[128,1024]{1,0:T(8,128)(2,1)S(1)}, bf16[128,1024]{1,0:T(8,128)(2,1)S(1)}, u32[]{:S(2)}, u32[]{:S(2)}) %collective-permute-start.2) | collective-permute-done | bytes 262176 | tf_op jit(solution)/shard_map/ppermute | solution.py:26
  292.5 13.1 %collective-permute-done.3 = bf16[128,1024]{1,0:T(8,128)(2,1)S(1)} collective-permute-done((bf16[128,1024]{1,0:T(8,128)(2,1)S(1)}, bf16[128,1024]{1,0:T(8,128)(2,1)S(1)}, u32[]{:S(2)}, u32[]{:S(2)}) %collective-permute-start.3) | collective-permute-done | bytes 262176 | tf_op jit(solution)/shard_map/ppermute | solution.py:26
  313.4 8.5 collective-permute-done.6
  321.9 12.2 %collective-permute-done.7 = bf16[128,1024]{1,0:T(8,128)(2,1)S(1)} collective-permute-done((bf16[128,1024]{1,0:T(8,128)(2,1)S(1)}, bf16[128,1024]{1,0:T(8,128)(2,1)S(1)}, u32[]{:S(2)}, u32[]{:S(2)}) %collective-permute-start.7) | collective-permute-done | bytes 262176 | tf_op jit(solution)/shard_map/ppermute | solution.py:26
  336.1 180.6 %while.17 = (s32[]{:T(128)}, bf16[4,128,8,128]{3,1,2,0:T(8,128)(2,1)}, bf16[4,128,8,128]{3,1,2,0:T(8,128)(2,1)}, f32[4,1152,128]{1,2,0:T(8,128)S(1)}, f32[4,1152...) while((s32[]{:T(128)}, ...), condition=%wide.region_4.5_spmd.clone, body=%wide.region_0.4_spmd.clone.sunk | while | flops 2449958400 | bytes 52865276 | solution.py:67
  346.7 12.1 %fusion.171 = f32[4,1152,128]{1,2,0:T(8,128)S(1)} fusion(f32[4,1152,128]{1,2,0:T(8,128)S(1)} %get-tuple-element.259, s32[]{:T(128)} %get-tuple-element.256, f32[128,8,1152]{2,0,1:T(8,128)} %fusion.169, bf16[4,128,8,128]{1,3,2,0:T(8,128)(2,1)} %get-tuple-element.274, f32[128,8,1152]{2,0,1:T(8,128)} %get-tuple-element.242, ...), kind=kOutput, calls=%fused_computation.17.clone.1 | convolution fusion | flops 310249600 | bytes 19735552 | tf_op jit(solution)/shard_map/while/body/eval_jaxpr/rhk,rhd->kd/dot_general | solution.py:53
  358.7 12.5 %fusion.170 = bf16[4,128,8,128]{3,1,2,0:T(8,128)(2,1)} fusion(bf16[4,128,8,128]{3,1,2,0:T(8,128)(2,1)} %get-tuple-element.258, s32[]{:T(128)} %get-tuple-element.256, f32[128,8,1152]{2,0,1:T(8,128)} %fusion.169, bf16[4,1152,128]{2,1,0:T(8,128)(2,1)} %get-tuple-element.275, f32[128,8,1152]{2,0,1:T(8,128)} %get-tuple-element.242, ...), kind=kOutput, calls=%fused_computation.28.clone.1 | convolution fusion | flops 310380672 | bytes 19440640 | tf_op jit(solution)/shard_map/while/body/eval_jaxpr/rhk,kd->rhd/dot_general | solution.py:50
  391.8 12.1 %fusion.171 = f32[4,1152,128]{1,2,0:T(8,128)S(1)} fusion(f32[4,1152,128]{1,2,0:T(8,128)S(1)} %get-tuple-element.259, s32[]{:T(128)} %get-tuple-element.256, f32[128,8,1152]{2,0,1:T(8,128)} %fusion.169, bf16[4,128,8,128]{1,3,2,0:T(8,128)(2,1)} %get-tuple-element.274, f32[128,8,1152]{2,0,1:T(8,128)} %get-tuple-element.242, ...), kind=kOutput, calls=%fused_computation.17.clone.1 | convolution fusion | flops 310249600 | bytes 19735552 | tf_op jit(solution)/shard_map/while/body/eval_jaxpr/rhk,rhd->kd/dot_general | solution.py:53
  403.9 12.5 %fusion.170 = bf16[4,128,8,128]{3,1,2,0:T(8,128)(2,1)} fusion(bf16[4,128,8,128]{3,1,2,0:T(8,128)(2,1)} %get-tuple-element.258, s32[]{:T(128)} %get-tuple-element.256, f32[128,8,1152]{2,0,1:T(8,128)} %fusion.169, bf16[4,1152,128]{2,1,0:T(8,128)(2,1)} %get-tuple-element.275, f32[128,8,1152]{2,0,1:T(8,128)} %get-tuple-element.242, ...), kind=kOutput, calls=%fused_computation.28.clone.1 | convolution fusion | flops 310380672 | bytes 19440640 | tf_op jit(solution)/shard_map/while/body/eval_jaxpr/rhk,kd->rhd/dot_general | solution.py:50
  437.0 12.1 %fusion.171 = f32[4,1152,128]{1,2,0:T(8,128)S(1)} fusion(f32[4,1152,128]{1,2,0:T(8,128)S(1)} %get-tuple-element.259, s32[]{:T(128)} %get-tuple-element.256, f32[128,8,1152]{2,0,1:T(8,128)} %fusion.169, bf16[4,128,8,128]{1,3,2,0:T(8,128)(2,1)} %get-tuple-element.274, f32[128,8,1152]{2,0,1:T(8,128)} %get-tuple-element.242, ...), kind=kOutput, calls=%fused_computation.17.clone.1 | convolution fusion | flops 310249600 | bytes 19735552 | tf_op jit(solution)/shard_map/while/body/eval_jaxpr/rhk,rhd->kd/dot_general | solution.py:53
  449.0 12.5 %fusion.170 = bf16[4,128,8,128]{3,1,2,0:T(8,128)(2,1)} fusion(bf16[4,128,8,128]{3,1,2,0:T(8,128)(2,1)} %get-tuple-element.258, s32[]{:T(128)} %get-tuple-element.256, f32[128,8,1152]{2,0,1:T(8,128)} %fusion.169, bf16[4,1152,128]{2,1,0:T(8,128)(2,1)} %get-tuple-element.275, f32[128,8,1152]{2,0,1:T(8,128)} %get-tuple-element.242, ...), kind=kOutput, calls=%fused_computation.28.clone.1 | convolution fusion | flops 310380672 | bytes 19440640 | tf_op jit(solution)/shard_map/while/body/eval_jaxpr/rhk,kd->rhd/dot_general | solution.py:50
  482.1 12.1 %fusion.171 = f32[4,1152,128]{1,2,0:T(8,128)S(1)} fusion(f32[4,1152,128]{1,2,0:T(8,128)S(1)} %get-tuple-element.259, s32[]{:T(128)} %get-tuple-element.256, f32[128,8,1152]{2,0,1:T(8,128)} %fusion.169, bf16[4,128,8,128]{1,3,2,0:T(8,128)(2,1)} %get-tuple-element.274, f32[128,8,1152]{2,0,1:T(8,128)} %get-tuple-element.242, ...), kind=kOutput, calls=%fused_computation.17.clone.1 | convolution fusion | flops 310249600 | bytes 19735552 | tf_op jit(solution)/shard_map/while/body/eval_jaxpr/rhk,rhd->kd/dot_general | solution.py:53
  494.2 12.5 %fusion.170 = bf16[4,128,8,128]{3,1,2,0:T(8,128)(2,1)} fusion(bf16[4,128,8,128]{3,1,2,0:T(8,128)(2,1)} %get-tuple-element.258, s32[]{:T(128)} %get-tuple-element.256, f32[128,8,1152]{2,0,1:T(8,128)} %fusion.169, bf16[4,1152,128]{2,1,0:T(8,128)(2,1)} %get-tuple-element.275, f32[128,8,1152]{2,0,1:T(8,128)} %get-tuple-element.242, ...), kind=kOutput, calls=%fused_computation.28.clone.1 | convolution fusion | flops 310380672 | bytes 19440640 | tf_op jit(solution)/shard_map/while/body/eval_jaxpr/rhk,kd->rhd/dot_general | solution.py:50
  536.8 17.9 %collective-permute-start.15 = (f32[128,1024]{0,1:T(8,128)S(1)}, f32[128,1024]{0,1:T(8,128)S(1)}, u32[]{:S(2)}, u32[]{:S(2)}) collective-permute-start(f32[128,1024]{0,1:T(8,128)S(1)} %get-tuple-element.160), channel_id=1, source_target_pairs={{8,0},{9,1},{10,2},{11,3},{12,4},{13,5},{14,6},{15,7},{16,8},{17,9... | collective-permute-start | bytes 1572872 | tf_op jit(solution)/shard_map/ppermute | solution.py:26
  554.7 15.7 %collective-permute-done.11 = f32[128,1024]{0,1:T(8,128)S(1)} collective-permute-done((f32[128,1024]{0,1:T(8,128)S(1)}, f32[128,1024]{0,1:T(8,128)S(1)}, u32[]{:S(2)}, u32[]{:S(2)}) %collective-permute-start.11) | collective-permute-done | bytes 524320 | tf_op jit(solution)/shard_map/ppermute | solution.py:26
  570.5 17.8 %collective-permute-start.8 = (f32[128,1024]{0,1:T(8,128)S(1)}, f32[128,1024]{0,1:T(8,128)S(1)}, u32[]{:S(2)}, u32[]{:S(2)}) collective-permute-start(f32[128,1024]{0,1:T(8,128)S(1)} %get-tuple-element.154), channel_id=1, source_target_pairs={{1,0},{2,1},{3,2},{4,3},{5,4},{6,5},{7,6},{8,7},{9,8},{10,9},{11,1... | collective-permute-start | bytes 1572872 | tf_op jit(solution)/shard_map/ppermute | solution.py:26
  588.3 13.7 %collective-permute-start.9 = (f32[128,1024]{0,1:T(8,128)S(1)}, f32[128,1024]{0,1:T(8,128)S(1)}, u32[]{:S(2)}, u32[]{:S(2)}) collective-permute-start(f32[128,1024]{0,1:T(8,128)S(1)} %get-tuple-element.155), channel_id=1, source_target_pairs={{2,0},{3,1},{4,2},{5,3},{6,4},{7,5},{8,6},{9,7},{10,8},{11,9},{12,... | collective-permute-start | bytes 1572872 | tf_op jit(solution)/shard_map/ppermute | solution.py:26
  602.0 32.7 %collective-permute-done.13 = f32[128,1024]{0,1:T(8,128)S(1)} collective-permute-done((f32[128,1024]{0,1:T(8,128)S(1)}, f32[128,1024]{0,1:T(8,128)S(1)}, u32[]{:S(2)}, u32[]{:S(2)}) %collective-permute-start.13) | collective-permute-done | bytes 524320 | tf_op jit(solution)/shard_map/ppermute | solution.py:26
  649.5 131.0 %all_to_all.19 = bf16[128,16,512]{0,2,1:T(8,128)(2,1)} all-to-all(bf16[128,16,512]{0,2,1:T(8,128)(2,1)} %bitcast.168), channel_id=1, replica_groups=mesh['seq'=16,'fsdp_0'=8,'fsdp_1'=2] {'fsdp_0','fsdp_1'}, dimensions={1} | all-to-all | bytes 4194304 | tf_op jit(solution)/shard_map/all_to_all | solution.py:84
  784.4 56.0 %all-gather.8.cloned.1.call-done = bf16[2048,1024]{0,1:T(8,128)(2,1)} async-done(((bf16[128,1024]{0,1:T(8,128)(2,1)}), bf16[2048,1024]{0,1:T(8,128)(2,1)}) %all-gather.8.cloned.1.call-update) | async-done | bytes 4194320 | tf_op jit(solution)/shard_map/all_gather | solution.py:115
  852.6 13.9 %convolution_convert_fusion.1 = bf16[128,8192]{1,0:T(8,128)(2,1)} fusion(bf16[8192,1024]{1,0:T(8,128)(2,1)} %all-gather.6.cloned.1.call-done, f32[128,1024]{0,1:T(8,128)} %copy-done.5, f32[128,1024]{0,1:T(8,128)} %copy-done.4, f32[128,1024]{0,1:T(8,128)} %copy-done.3, f32[128,1024]{0,1:T(8,128)} %copy-done.2, f32[128,1024]{0,1:T(8,128)S(1)} %collective-permute-done.11, ...), kind=kOutput, calls=%fused_computation.83 | convolution fusion | flops 2150891520 | bytes 27787272 | tf_op jit(solution)/shard_map/dot_general | solution.py:110
  866.5 136.3 %all-reduce.2.cloned.1.call-done = f32[512,1024]{0,1:T(8,128)} async-done(((f32[512,1024]{0,1:T(8,128)}), f32[512,1024]{0,1:T(8,128)}) %all-reduce.2.cloned.1.call-update) | async-done | bytes 2097168 | tf_op jit(solution)/shard_map/psum | solution.py:119
  (104 shorter events, 193.9 us)
Async XLA Ops:
  7.2 45.2 %all-gather.4.cloned.1.call-start = ((), (), s32[]{:S(2)}) async-start(), calls=%async_computation.1 | async-start | bytes 3145728 | tf_op jit(solution)/shard_map/all_gather | solution.py:19
  10.0 218.0 %copy-start.1 = (bf16[128,8192]{1,0:T(8,128)(2,1)S(1)}, bf16[128,8192]{1,0:T(8,128)(2,1)}, u32[]{:S(2)}) copy-start(bf16[128,8192]{1,0:T(8,128)(2,1)} %param.7) | copy-start | bytes 6291460
  10.0 218.0 %all-gather.6.cloned.1.call-start = ((), (), s32[]{:S(2)}) async-start(), calls=%async_computation.2 | async-start | bytes 18874368 | tf_op jit(solution)/shard_map/all_gather | solution.py:19
  52.4 788.0 %all-gather.8.cloned.1.call-start = ((), (), s32[]{:S(2)}) async-start(), calls=%async_computation.3 | async-start | bytes 4456448 | tf_op jit(solution)/shard_map/all_gather | solution.py:115
  236.1 26.6 %collective-permute-start = (bf16[128,1024]{1,0:T(8,128)(2,1)S(1)}, bf16[128,1024]{1,0:T(8,128)(2,1)}, u32[]{:S(2)}, u32[]{:S(2)}) collective-permute-start(bf16[128,1024]{1,0:T(8,128)(2,1)S(1)} %fusion.100), channel_id=1, source_target_pairs={{0,8},{1,9},{2,10},{3,11},{4,12},{5,13},{6,14},{7,15},{8,16},{9,17... | collective-permute-start | bytes 786440 | tf_op jit(solution)/shard_map/ppermute | solution.py:26
  240.8 28.2 %collective-permute-start.1 = (bf16[128,1024]{1,0:T(8,128)(2,1)S(1)}, bf16[128,1024]{1,0:T(8,128)(2,1)S(1)}, u32[]{:S(2)}, u32[]{:S(2)}) collective-permute-start(bf16[128,1024]{1,0:T(8,128)(2,1)S(1)} %fusion.100), channel_id=1, source_target_pairs={{0,7},{1,8},{2,9},{3,10},{4,11},{5,12},{6,13},{7,14},{8,15},{9,16}... | collective-permute-start | bytes 786440 | tf_op jit(solution)/shard_map/ppermute | solution.py:26
  245.0 45.6 %collective-permute-start.2 = (bf16[128,1024]{1,0:T(8,128)(2,1)S(1)}, bf16[128,1024]{1,0:T(8,128)(2,1)S(1)}, u32[]{:S(2)}, u32[]{:S(2)}) collective-permute-start(bf16[128,1024]{1,0:T(8,128)(2,1)S(1)} %fusion.100), channel_id=1, source_target_pairs={{0,6},{1,7},{2,8},{3,9},{4,10},{5,11},{6,12},{7,13},{8,14},{9,15},... | collective-permute-start | bytes 786440 | tf_op jit(solution)/shard_map/ppermute | solution.py:26
  255.4 50.2 %collective-permute-start.3 = (bf16[128,1024]{1,0:T(8,128)(2,1)S(1)}, bf16[128,1024]{1,0:T(8,128)(2,1)S(1)}, u32[]{:S(2)}, u32[]{:S(2)}) collective-permute-start(bf16[128,1024]{1,0:T(8,128)(2,1)S(1)} %fusion.100), channel_id=1, source_target_pairs={{0,5},{1,6},{2,7},{3,8},{4,9},{5,10},{6,11},{7,12},{8,13},{9,14},{... | collective-permute-start | bytes 786440 | tf_op jit(solution)/shard_map/ppermute | solution.py:26
  260.3 45.2 %collective-permute-start.4 = (bf16[128,1024]{1,0:T(8,128)(2,1)S(1)}, bf16[128,1024]{1,0:T(8,128)(2,1)S(1)}, u32[]{:S(2)}, u32[]{:S(2)}) collective-permute-start(bf16[128,1024]{1,0:T(8,128)(2,1)S(1)} %fusion.100), channel_id=1, source_target_pairs={{0,4},{1,5},{2,6},{3,7},{4,8},{5,9},{6,10},{7,11},{8,12},{9,13},{1... | collective-permute-start | bytes 786440 | tf_op jit(solution)/shard_map/ppermute | solution.py:26
  262.7 50.7 %collective-permute-start.5 = (bf16[128,1024]{1,0:T(8,128)(2,1)S(1)}, bf16[128,1024]{1,0:T(8,128)(2,1)S(1)}, u32[]{:S(2)}, u32[]{:S(2)}) collective-permute-start(bf16[128,1024]{1,0:T(8,128)(2,1)S(1)} %fusion.100), channel_id=1, source_target_pairs={{0,3},{1,4},{2,5},{3,6},{4,7},{5,8},{6,9},{7,10},{8,11},{9,12},{10... | collective-permute-start | bytes 786440 | tf_op jit(solution)/shard_map/ppermute | solution.py:26
  269.0 52.8 %collective-permute-start.6 = (bf16[128,1024]{1,0:T(8,128)(2,1)S(1)}, bf16[128,1024]{1,0:T(8,128)(2,1)S(1)}, u32[]{:S(2)}, u32[]{:S(2)}) collective-permute-start(bf16[128,1024]{1,0:T(8,128)(2,1)S(1)} %fusion.100), channel_id=1, source_target_pairs={{0,2},{1,3},{2,4},{3,5},{4,6},{5,7},{6,8},{7,9},{8,10},{9,11},{10,... | collective-permute-start | bytes 786440 | tf_op jit(solution)/shard_map/ppermute | solution.py:26
  290.5 43.6 %collective-permute-start.7 = (bf16[128,1024]{1,0:T(8,128)(2,1)S(1)}, bf16[128,1024]{1,0:T(8,128)(2,1)S(1)}, u32[]{:S(2)}, u32[]{:S(2)}) collective-permute-start(bf16[128,1024]{1,0:T(8,128)(2,1)S(1)} %fusion.100), channel_id=1, source_target_pairs={{0,1},{1,2},{2,3},{3,4},{4,5},{5,6},{6,7},{7,8},{8,9},{9,10},{10,1... | collective-permute-start | bytes 786440 | tf_op jit(solution)/shard_map/ppermute | solution.py:26
  516.7 127.6 %copy-start = (f32[4,1152,128]{1,2,0:T(8,128)S(1)}, f32[4,1152,128]{1,2,0:T(8,128)}, u32[]{:S(2)}) copy-start(f32[4,1152,128]{1,2,0:T(8,128)} %get-tuple-element.62) | copy-start | bytes 7077892
  518.7 18.1 %collective-permute-start.10 = (f32[128,1024]{0,1:T(8,128)S(1)}, f32[128,1024]{0,1:T(8,128)S(1)}, u32[]{:S(2)}, u32[]{:S(2)}) collective-permute-start(f32[128,1024]{0,1:T(8,128)S(1)} %get-tuple-element.156), channel_id=1, source_target_pairs={{3,0},{4,1},{5,2},{6,3},{7,4},{8,5},{9,6},{10,7},{11,8},{12,9},{13... | collective-permute-start | bytes 1572872 | tf_op jit(solution)/shard_map/ppermute | solution.py:26
  520.6 49.9 %collective-permute-start.11 = (f32[128,1024]{0,1:T(8,128)S(1)}, f32[128,1024]{0,1:T(8,128)S(1)}, u32[]{:S(2)}, u32[]{:S(2)}) collective-permute-start(f32[128,1024]{0,1:T(8,128)S(1)} %get-tuple-element.157), channel_id=1, source_target_pairs={{4,0},{5,1},{6,2},{7,3},{8,4},{9,5},{10,6},{11,7},{12,8},{13,9},{1... | collective-permute-start | bytes 1572872 | tf_op jit(solution)/shard_map/ppermute | solution.py:26
  525.2 63.1 %collective-permute-start.12 = (f32[128,1024]{0,1:T(8,128)S(1)}, f32[128,1024]{0,1:T(8,128)S(1)}, u32[]{:S(2)}, u32[]{:S(2)}) collective-permute-start(f32[128,1024]{0,1:T(8,128)S(1)} %get-tuple-element.158), channel_id=1, source_target_pairs={{5,0},{6,1},{7,2},{8,3},{9,4},{10,5},{11,6},{12,7},{13,8},{14,9},{... | collective-permute-start | bytes 1572872 | tf_op jit(solution)/shard_map/ppermute | solution.py:26
  531.0 103.8 %collective-permute-start.13 = (f32[128,1024]{0,1:T(8,128)S(1)}, f32[128,1024]{0,1:T(8,128)S(1)}, u32[]{:S(2)}, u32[]{:S(2)}) collective-permute-start(f32[128,1024]{0,1:T(8,128)S(1)} %get-tuple-element.159), channel_id=1, source_target_pairs={{6,0},{7,1},{8,2},{9,3},{10,4},{11,5},{12,6},{13,7},{14,8},{15,9},... | collective-permute-start | bytes 1572872 | tf_op jit(solution)/shard_map/ppermute | solution.py:26
  533.0 109.3 %collective-permute-start.14 = (f32[128,1024]{0,1:T(8,128)S(1)}, f32[128,1024]{0,1:T(8,128)S(1)}, u32[]{:S(2)}, u32[]{:S(2)}) collective-permute-start(f32[128,1024]{0,1:T(8,128)S(1)} %get-tuple-element.161), channel_id=1, source_target_pairs={{7,0},{8,1},{9,2},{10,3},{11,4},{12,5},{13,6},{14,7},{15,8},{16,9}... | collective-permute-start | bytes 1572872 | tf_op jit(solution)/shard_map/ppermute | solution.py:26
  536.8 105.5 %collective-permute-start.15 = (f32[128,1024]{0,1:T(8,128)S(1)}, f32[128,1024]{0,1:T(8,128)S(1)}, u32[]{:S(2)}, u32[]{:S(2)}) collective-permute-start(f32[128,1024]{0,1:T(8,128)S(1)} %get-tuple-element.160), channel_id=1, source_target_pairs={{8,0},{9,1},{10,2},{11,3},{12,4},{13,5},{14,6},{15,7},{16,8},{17,9... | collective-permute-start | bytes 1572872 | tf_op jit(solution)/shard_map/ppermute | solution.py:26
  570.5 71.8 %collective-permute-start.8 = (f32[128,1024]{0,1:T(8,128)S(1)}, f32[128,1024]{0,1:T(8,128)S(1)}, u32[]{:S(2)}, u32[]{:S(2)}) collective-permute-start(f32[128,1024]{0,1:T(8,128)S(1)} %get-tuple-element.154), channel_id=1, source_target_pairs={{1,0},{2,1},{3,2},{4,3},{5,4},{6,5},{7,6},{8,7},{9,8},{10,9},{11,1... | collective-permute-start | bytes 1572872 | tf_op jit(solution)/shard_map/ppermute | solution.py:26
  588.3 54.0 %copy-start.2 = (f32[128,1024]{0,1:T(8,128)}, f32[128,1024]{0,1:T(8,128)S(1)}, u32[]{:S(2)}) copy-start(f32[128,1024]{0,1:T(8,128)S(1)} %collective-permute-done.12) | copy-start | bytes 1572868
  588.3 54.0 %collective-permute-start.9 = (f32[128,1024]{0,1:T(8,128)S(1)}, f32[128,1024]{0,1:T(8,128)S(1)}, u32[]{:S(2)}, u32[]{:S(2)}) collective-permute-start(f32[128,1024]{0,1:T(8,128)S(1)} %get-tuple-element.155), channel_id=1, source_target_pairs={{2,0},{3,1},{4,2},{5,3},{6,4},{7,5},{8,6},{9,7},{10,8},{11,9},{12,... | collective-permute-start | bytes 1572872 | tf_op jit(solution)/shard_map/ppermute | solution.py:26
  634.7 7.6 copy-start.3
  645.4 357.4 %all-reduce.2.cloned.1.call-start = ((), (), s32[]{:S(2)}) async-start(), calls=%async_computation.4 | async-start | bytes 4194304 | tf_op jit(solution)/shard_map/psum | solution.py:119
  (6 other events, 8.4 us)
Sparse Core Ops, SparseCore 0:
  10.4 41.9 all-gather.3
  54.2 173.7 all-gather.5
  645.5 194.9 all-gather.7
  847.1 155.5 all-reduce.1
where the time goes:
time: 1010 us
  waiting for transfers between devices  529 us (52%)
  matrix products  206 us (20%)
  blocking collectives  131 us (13%)
  starting transfers between devices  97.6 us (10%)
  local copies, waits for them, and re-layouts  27.1 us (3%)
  between operations  14.2 us (1%)
    all_gather x2, waiting for transfers between devices, gather_axes(): nearer = lax.all_gather(value, axes[-1], axis=dim, tiled=True)  218 us
    psum x1, waiting for transfers between devices, body(): weight_grad = lax.psum(shard_grad, 'seq')  136 us
    all_to_all x1, blocking collectives, body(): lax.all_to_all(hidden, FSDP, split_axis=1, concat_axis=0, tiled=True)  131 us
    ppermute x16, waiting for transfers between devices, shifted(): return lax.ppermute(block, axis, route)  118 us
    ppermute x16, starting transfers between devices, shifted(): return lax.ppermute(block, axis, route)  97.5 us
    all_gather x1, waiting for transfers between devices, body(): lax.all_gather(all_grad, FSDP, axis=0, tiled=True)  56 us
    dot_general x4, matrix products, attend_group(): jnp.einsum('rhk,kd->rhd', dscores, kgrp, preferred_element_type=jnp.float32)  50.1 us
    dot_general x4, matrix products, attend_group(): jnp.einsum('rhk,rhd->kd', dscores, qgrp, preferred_element_type=jnp.float32)  48.3 us
  transfers between devices with their start and end apart: 20, of which 13 were waited for; matrix products, arithmetic and copies ran while one was open for 3% of the time, Pallas kernels for 0%

commit v1 on v0

--- a/solution.py
+++ b/solution.py
@@ -116,7 +116,7 @@
         (((0,), (0,)), ((), ())),
         preferred_element_type=jnp.float32,
     )
-    weight_grad = lax.psum(shard_grad, "seq")
+    weight_grad = jnp.sum(lax.all_gather(shard_grad, "seq"), axis=0)
     return (attn_out, grad_queries, grad_hidden, weight_grad)
 
 

time: 1010 us -> 1110 us (1.099); the launches traced: 1010 us -> 1100 us
  waiting for transfers between devices: 529 us -> 596 us
  local copies, waits for them, and re-layouts: 27.1 us -> 60.9 us
  blocking collectives: 131 us -> 112 us
    all_gather x0 -> x1, waiting for transfers between devices: none -> 182 us  [body(): weight_grad = jnp.sum(lax.all_gather(shard_grad, 'seq'), axis=0)]
    psum x1 -> x0, waiting for transfers between devices: 136 us -> none  [body(): weight_grad = lax.psum(shard_grad, 'seq')]
    unnamed x35 -> x36, local copies, waits for them, and re-layouts: 18 us -> 51.9 us
    ppermute x16, waiting for transfers between devices: 118 us -> 143 us  [shifted(): return lax.ppermute(block, axis, route)]
    all_to_all x1, blocking collectives: 131 us -> 112 us  [body(): lax.all_to_all(hidden, FSDP, split_axis=1, concat_axis=0, tiled=True)]
  transfers between devices with their start and end apart: 20 -> 20, of which waited for: 13 -> 12; matrix products, arithmetic and copies ran while one was open for 3% -> 3% of each run, Pallas kernels for 0% -> 0%
where the time goes in v1:
time: 1110 us; the launch traced here: 1100 us
  waiting for transfers between devices  596 us (54%)
  matrix products  206 us (19%)
  blocking collectives  112 us (10%)
  starting transfers between devices  93.6 us (8%)
  local copies, waits for them, and re-layouts  60.9 us (5%)
  other arithmetic  16.4 us (1%)
  between operations  14.4 us (1%)
    all_gather x2, waiting for transfers between devices, gather_axes(): nearer = lax.all_gather(value, axes[-1], axis=dim, tiled=True)  218 us
    all_gather x1, waiting for transfers between devices, body(): weight_grad = jnp.sum(lax.all_gather(shard_grad, 'seq'), axis=0)  182 us
    ppermute x16, waiting for transfers between devices, shifted(): return lax.ppermute(block, axis, route)  143 us
    all_to_all x1, blocking collectives, body(): lax.all_to_all(hidden, FSDP, split_axis=1, concat_axis=0, tiled=True)  112 us
    ppermute x16, starting transfers between devices, shifted(): return lax.ppermute(block, axis, route)  93.4 us
    all_gather x1, waiting for transfers between devices, body(): lax.all_gather(all_grad, FSDP, axis=0, tiled=True)  53.9 us
    unnamed x36, local copies, waits for them, and re-layouts  51.9 us
    dot_general x4, matrix products, attend_group(): jnp.einsum('rhk,rhd->kd', dscores, qgrp, preferred_element_type=jnp.float32)  51.8 us
  transfers between devices with their start and end apart: 20, of which 12 were waited for; matrix products, arithmetic and copies ran while one was open for 3% of the time, Pallas kernels for 0%

profile of v1, /device:TPU:1, one launch (start us, length us, event | category | flops | bytes accessed | tf_op | source)
XLA Modules:
  0.0 1101.0 jit_solution(3516511837866165120)
XLA Ops:
  10.0 42.4 %all-gather.6.cloned.1.call-done = bf16[1024,1024]{1,0:T(8,128)(2,1)} async-done(((bf16[512,1024]{1,0:T(8,128)(2,1)}), bf16[1024,1024]{1,0:T(8,128)(2,1)}) %all-gather.6.cloned.1.call-update) | async-done | bytes 2097168 | tf_op jit(solution)/shard_map/all_gather | solution.py:19
  52.5 175.5 %all-gather.8.cloned.1.call-done = bf16[8192,1024]{1,0:T(8,128)(2,1)} async-done(((bf16[1024,1024]{1,0:T(8,128)(2,1)}), bf16[8192,1024]{1,0:T(8,128)(2,1)}) %all-gather.8.cloned.1.call-update) | async-done | bytes 16777232 | tf_op jit(solution)/shard_map/all_gather | solution.py:19
  272.2 15.9 %collective-permute-done.2 = bf16[128,1024]{1,0:T(8,128)(2,1)S(1)} collective-permute-done((bf16[128,1024]{1,0:T(8,128)(2,1)S(1)}, bf16[128,1024]{1,0:T(8,128)(2,1)S(1)}, u32[]{:S(2)}, u32[]{:S(2)}) %collective-permute-start.2) | collective-permute-done | bytes 262176 | tf_op jit(solution)/shard_map/ppermute | solution.py:26
  290.1 26.5 %collective-permute-done.3 = bf16[128,1024]{1,0:T(8,128)(2,1)S(1)} collective-permute-done((bf16[128,1024]{1,0:T(8,128)(2,1)S(1)}, bf16[128,1024]{1,0:T(8,128)(2,1)S(1)}, u32[]{:S(2)}, u32[]{:S(2)}) %collective-permute-start.3) | collective-permute-done | bytes 262176 | tf_op jit(solution)/shard_map/ppermute | solution.py:26
  323.6 181.8 %while.17 = (s32[]{:T(128)}, bf16[4,128,8,128]{3,1,2,0:T(8,128)(2,1)}, bf16[4,128,8,128]{3,1,2,0:T(8,128)(2,1)}, f32[4,1152,128]{1,2,0:T(8,128)}, f32[4,1152,128...) while((s32[]{:T(128)}, ...), condition=%wide.region_4.5_spmd.clone, body=%wide.region_0.4_spmd.clone.sunk | while | flops 2449958400 | bytes 52865284 | solution.py:67
  334.6 12.6 %fusion.170 = bf16[4,128,8,128]{3,1,2,0:T(8,128)(2,1)} fusion(bf16[4,128,8,128]{3,1,2,0:T(8,128)(2,1)} %get-tuple-element.262, s32[]{:T(128)S(6)} %copy.95, f32[128,8,1152]{2,0,1:T(8,128)} %fusion.169, bf16[4,1152,128]{2,1,0:T(8,128)(2,1)} %get-tuple-element.279, f32[128,8,1152]{2,0,1:T(8,128)} %get-tuple-element.246, f32[128,8]{0,1:T(8,128)} %get-tuple-element.245), kind=kOutput, calls=%fused_computation.28.clone.1 | convolution fusion | flops 310380672 | bytes 19440640 | tf_op jit(solution)/shard_map/while/body/eval_jaxpr/rhk,kd->rhd/dot_general | solution.py:50
  347.2 12.9 %fusion.171 = f32[4,1152,128]{1,2,0:T(8,128)} fusion(f32[4,1152,128]{1,2,0:T(8,128)} %get-tuple-element.263, s32[]{:T(128)S(6)} %copy.95, f32[128,8,1152]{2,0,1:T(8,128)} %fusion.169, bf16[4,128,8,128]{1,3,2,0:T(8,128)(2,1)} %get-tuple-element.278, f32[128,8,1152]{2,0,1:T(8,128)} %get-tuple-element.246, f32[128,8]{0,1:T(8,128)} %get-tuple-element.245), kind=kOutput, calls=%fused_computation.17.clone.1 | convolution fusion | flops 310249600 | bytes 19735552 | tf_op jit(solution)/shard_map/while/body/eval_jaxpr/rhk,rhd->kd/dot_general | solution.py:53
  379.9 12.6 %fusion.170 = bf16[4,128,8,128]{3,1,2,0:T(8,128)(2,1)} fusion(bf16[4,128,8,128]{3,1,2,0:T(8,128)(2,1)} %get-tuple-element.262, s32[]{:T(128)S(6)} %copy.95, f32[128,8,1152]{2,0,1:T(8,128)} %fusion.169, bf16[4,1152,128]{2,1,0:T(8,128)(2,1)} %get-tuple-element.279, f32[128,8,1152]{2,0,1:T(8,128)} %get-tuple-element.246, f32[128,8]{0,1:T(8,128)} %get-tuple-element.245), kind=kOutput, calls=%fused_computation.28.clone.1 | convolution fusion | flops 310380672 | bytes 19440640 | tf_op jit(solution)/shard_map/while/body/eval_jaxpr/rhk,kd->rhd/dot_general | solution.py:50
  392.4 12.9 %fusion.171 = f32[4,1152,128]{1,2,0:T(8,128)} fusion(f32[4,1152,128]{1,2,0:T(8,128)} %get-tuple-element.263, s32[]{:T(128)S(6)} %copy.95, f32[128,8,1152]{2,0,1:T(8,128)} %fusion.169, bf16[4,128,8,128]{1,3,2,0:T(8,128)(2,1)} %get-tuple-element.278, f32[128,8,1152]{2,0,1:T(8,128)} %get-tuple-element.246, f32[128,8]{0,1:T(8,128)} %get-tuple-element.245), kind=kOutput, calls=%fused_computation.17.clone.1 | convolution fusion | flops 310249600 | bytes 19735552 | tf_op jit(solution)/shard_map/while/body/eval_jaxpr/rhk,rhd->kd/dot_general | solution.py:53
  425.1 12.6 %fusion.170 = bf16[4,128,8,128]{3,1,2,0:T(8,128)(2,1)} fusion(bf16[4,128,8,128]{3,1,2,0:T(8,128)(2,1)} %get-tuple-element.262, s32[]{:T(128)S(6)} %copy.95, f32[128,8,1152]{2,0,1:T(8,128)} %fusion.169, bf16[4,1152,128]{2,1,0:T(8,128)(2,1)} %get-tuple-element.279, f32[128,8,1152]{2,0,1:T(8,128)} %get-tuple-element.246, f32[128,8]{0,1:T(8,128)} %get-tuple-element.245), kind=kOutput, calls=%fused_computation.28.clone.1 | convolution fusion | flops 310380672 | bytes 19440640 | tf_op jit(solution)/shard_map/while/body/eval_jaxpr/rhk,kd->rhd/dot_general | solution.py:50
  437.8 13.0 %fusion.171 = f32[4,1152,128]{1,2,0:T(8,128)} fusion(f32[4,1152,128]{1,2,0:T(8,128)} %get-tuple-element.263, s32[]{:T(128)S(6)} %copy.95, f32[128,8,1152]{2,0,1:T(8,128)} %fusion.169, bf16[4,128,8,128]{1,3,2,0:T(8,128)(2,1)} %get-tuple-element.278, f32[128,8,1152]{2,0,1:T(8,128)} %get-tuple-element.246, f32[128,8]{0,1:T(8,128)} %get-tuple-element.245), kind=kOutput, calls=%fused_computation.17.clone.1 | convolution fusion | flops 310249600 | bytes 19735552 | tf_op jit(solution)/shard_map/while/body/eval_jaxpr/rhk,rhd->kd/dot_general | solution.py:53
  470.5 12.6 %fusion.170 = bf16[4,128,8,128]{3,1,2,0:T(8,128)(2,1)} fusion(bf16[4,128,8,128]{3,1,2,0:T(8,128)(2,1)} %get-tuple-element.262, s32[]{:T(128)S(6)} %copy.95, f32[128,8,1152]{2,0,1:T(8,128)} %fusion.169, bf16[4,1152,128]{2,1,0:T(8,128)(2,1)} %get-tuple-element.279, f32[128,8,1152]{2,0,1:T(8,128)} %get-tuple-element.246, f32[128,8]{0,1:T(8,128)} %get-tuple-element.245), kind=kOutput, calls=%fused_computation.28.clone.1 | convolution fusion | flops 310380672 | bytes 19440640 | tf_op jit(solution)/shard_map/while/body/eval_jaxpr/rhk,kd->rhd/dot_general | solution.py:50
  483.1 12.9 %fusion.171 = f32[4,1152,128]{1,2,0:T(8,128)} fusion(f32[4,1152,128]{1,2,0:T(8,128)} %get-tuple-element.263, s32[]{:T(128)S(6)} %copy.95, f32[128,8,1152]{2,0,1:T(8,128)} %fusion.169, bf16[4,128,8,128]{1,3,2,0:T(8,128)(2,1)} %get-tuple-element.278, f32[128,8,1152]{2,0,1:T(8,128)} %get-tuple-element.246, f32[128,8]{0,1:T(8,128)} %get-tuple-element.245), kind=kOutput, calls=%fused_computation.17.clone.1 | convolution fusion | flops 310249600 | bytes 19735552 | tf_op jit(solution)/shard_map/while/body/eval_jaxpr/rhk,rhd->kd/dot_general | solution.py:53
  507.4 14.3 %collective-permute-start.8 = (f32[128,1024]{0,1:T(8,128)S(1)}, f32[128,1024]{0,1:T(8,128)S(1)}, u32[]{:S(2)}, u32[]{:S(2)}) collective-permute-start(f32[128,1024]{0,1:T(8,128)S(1)} %get-tuple-element.158), channel_id=1, source_target_pairs={{1,0},{2,1},{3,2},{4,3},{5,4},{6,5},{7,6},{8,7},{9,8},{10,9},{11,1... | collective-permute-start | bytes 1572872 | tf_op jit(solution)/shard_map/ppermute | solution.py:26
  541.1 23.3 %collective-permute-start.15 = (f32[128,1024]{0,1:T(8,128)S(1)}, f32[128,1024]{0,1:T(8,128)S(1)}, u32[]{:S(2)}, u32[]{:S(2)}) collective-permute-start(f32[128,1024]{0,1:T(8,128)S(1)} %get-tuple-element.164), channel_id=1, source_target_pairs={{8,0},{9,1},{10,2},{11,3},{12,4},{13,5},{14,6},{15,7},{16,8},{17,9... | collective-permute-start | bytes 1572872 | tf_op jit(solution)/shard_map/ppermute | solution.py:26
  570.0 9.4 collective-permute-done.11
  579.4 16.6 %collective-permute-done.12 = f32[128,1024]{0,1:T(8,128)S(1)} collective-permute-done((f32[128,1024]{0,1:T(8,128)S(1)}, f32[128,1024]{0,1:T(8,128)S(1)}, u32[]{:S(2)}, u32[]{:S(2)}) %collective-permute-start.12) | collective-permute-done | bytes 524320 | tf_op jit(solution)/shard_map/ppermute | solution.py:26
  596.0 58.5 %collective-permute-done.13 = f32[128,1024]{0,1:T(8,128)S(1)} collective-permute-done((f32[128,1024]{0,1:T(8,128)S(1)}, f32[128,1024]{0,1:T(8,128)S(1)}, u32[]{:S(2)}, u32[]{:S(2)}) %collective-permute-start.13) | collective-permute-done | bytes 524320 | tf_op jit(solution)/shard_map/ppermute | solution.py:26
  654.5 10.3 collective-permute-done.14
  670.8 112.4 %all_to_all.19 = bf16[128,16,512]{0,2,1:T(8,128)(2,1)} all-to-all(bf16[128,16,512]{0,2,1:T(8,128)(2,1)} %bitcast.174), channel_id=1, replica_groups=mesh['seq'=16,'fsdp_0'=8,'fsdp_1'=2] {'fsdp_0','fsdp_1'}, dimensions={1} | all-to-all | bytes 4194304 | tf_op jit(solution)/shard_map/all_to_all | solution.py:84
  787.1 53.9 %all-gather.10.cloned.1.call-done = bf16[2048,1024]{0,1:T(8,128)(2,1)} async-done(((bf16[128,1024]{0,1:T(8,128)(2,1)}), bf16[2048,1024]{0,1:T(8,128)(2,1)}) %all-gather.10.cloned.1.call-update) | async-done | bytes 4194320 | tf_op jit(solution)/shard_map/all_gather | solution.py:115
  853.1 13.9 %convolution_convert_fusion.1 = bf16[128,8192]{1,0:T(8,128)(2,1)} fusion(bf16[8192,1024]{1,0:T(8,128)(2,1)} %all-gather.8.cloned.1.call-done, f32[128,1024]{0,1:T(8,128)} %copy-done.6, f32[128,1024]{0,1:T(8,128)} %copy-done.7, f32[128,1024]{0,1:T(8,128)} %copy-done.5, f32[128,1024]{0,1:T(8,128)} %copy-done.4, f32[128,1024]{0,1:T(8,128)} %copy-done.3, ...), kind=kOutput, calls=%fused_computation.84 | convolution fusion | flops 2150891520 | bytes 27787272 | tf_op jit(solution)/shard_map/dot_general | solution.py:110
  867.1 181.8 %all-gather.12.cloned.1.call-done = f32[8192,1024]{0,1:T(8,128)} async-done(((f32[512,1024]{0,1:T(8,128)}), f32[8192,1024]{0,1:T(8,128)}) %all-gather.12.cloned.1.call-update) | async-done | bytes 33554448 | tf_op jit(solution)/shard_map/all_gather | solution.py:119
  1048.9 35.1 %copy.70 = f32[128,8,16,512]{3,2,1,0:T(8,128)S(1)} copy(f32[128,8,16,512]{3,1,2,0:T(8,128)} %bitcast.165) | data formatting | bytes 67108864
  (106 shorter events, 193.7 us)
Async XLA Ops:
  7.2 45.2 %all-gather.6.cloned.1.call-start = ((), (), s32[]{:S(2)}) async-start(), calls=%async_computation.1 | async-start | bytes 3145728 | tf_op jit(solution)/shard_map/all_gather | solution.py:19
  10.0 218.0 %copy-start.1 = (bf16[128,8192]{1,0:T(8,128)(2,1)S(1)}, bf16[128,8192]{1,0:T(8,128)(2,1)}, u32[]{:S(2)}) copy-start(bf16[128,8192]{1,0:T(8,128)(2,1)} %param.7) | copy-start | bytes 6291460
  10.0 218.0 %all-gather.8.cloned.1.call-start = ((), (), s32[]{:S(2)}) async-start(), calls=%async_computation.2 | async-start | bytes 18874368 | tf_op jit(solution)/shard_map/all_gather | solution.py:19
  52.4 788.6 %all-gather.10.cloned.1.call-start = ((), (), s32[]{:S(2)}) async-start(), calls=%async_computation.3 | async-start | bytes 4456448 | tf_op jit(solution)/shard_map/all_gather | solution.py:115
  236.1 26.5 %collective-permute-start = (bf16[128,1024]{1,0:T(8,128)(2,1)S(1)}, bf16[128,1024]{1,0:T(8,128)(2,1)}, u32[]{:S(2)}, u32[]{:S(2)}) collective-permute-start(bf16[128,1024]{1,0:T(8,128)(2,1)S(1)} %fusion.100), channel_id=1, source_target_pairs={{0,8},{1,9},{2,10},{3,11},{4,12},{5,13},{6,14},{7,15},{8,16},{9,17... | collective-permute-start | bytes 786440 | tf_op jit(solution)/shard_map/ppermute | solution.py:26
  240.8 26.8 %collective-permute-start.1 = (bf16[128,1024]{1,0:T(8,128)(2,1)S(1)}, bf16[128,1024]{1,0:T(8,128)(2,1)}, u32[]{:S(2)}, u32[]{:S(2)}) collective-permute-start(bf16[128,1024]{1,0:T(8,128)(2,1)S(1)} %fusion.100), channel_id=1, source_target_pairs={{0,7},{1,8},{2,9},{3,10},{4,11},{5,12},{6,13},{7,14},{8,15},{9,16}... | collective-permute-start | bytes 786440 | tf_op jit(solution)/shard_map/ppermute | solution.py:26
  245.0 43.2 %collective-permute-start.2 = (bf16[128,1024]{1,0:T(8,128)(2,1)S(1)}, bf16[128,1024]{1,0:T(8,128)(2,1)S(1)}, u32[]{:S(2)}, u32[]{:S(2)}) collective-permute-start(bf16[128,1024]{1,0:T(8,128)(2,1)S(1)} %fusion.100), channel_id=1, source_target_pairs={{0,6},{1,7},{2,8},{3,9},{4,10},{5,11},{6,12},{7,13},{8,14},{9,15},... | collective-permute-start | bytes 786440 | tf_op jit(solution)/shard_map/ppermute | solution.py:26
  255.4 66.2 %collective-permute-start.7 = (bf16[128,1024]{1,0:T(8,128)(2,1)S(1)}, bf16[128,1024]{1,0:T(8,128)(2,1)S(1)}, u32[]{:S(2)}, u32[]{:S(2)}) collective-permute-start(bf16[128,1024]{1,0:T(8,128)(2,1)S(1)} %fusion.100), channel_id=1, source_target_pairs={{0,1},{1,2},{2,3},{3,4},{4,5},{5,6},{6,7},{7,8},{8,9},{9,10},{10,1... | collective-permute-start | bytes 786440 | tf_op jit(solution)/shard_map/ppermute | solution.py:26
  260.7 60.9 %collective-permute-start.6 = (bf16[128,1024]{1,0:T(8,128)(2,1)S(1)}, bf16[128,1024]{1,0:T(8,128)(2,1)S(1)}, u32[]{:S(2)}, u32[]{:S(2)}) collective-permute-start(bf16[128,1024]{1,0:T(8,128)(2,1)S(1)} %fusion.100), channel_id=1, source_target_pairs={{0,2},{1,3},{2,4},{3,5},{4,6},{5,7},{6,8},{7,9},{8,10},{9,11},{10,... | collective-permute-start | bytes 786440 | tf_op jit(solution)/shard_map/ppermute | solution.py:26
  262.6 54.0 %collective-permute-start.3 = (bf16[128,1024]{1,0:T(8,128)(2,1)S(1)}, bf16[128,1024]{1,0:T(8,128)(2,1)S(1)}, u32[]{:S(2)}, u32[]{:S(2)}) collective-permute-start(bf16[128,1024]{1,0:T(8,128)(2,1)S(1)} %fusion.100), channel_id=1, source_target_pairs={{0,5},{1,6},{2,7},{3,8},{4,9},{5,10},{6,11},{7,12},{8,13},{9,14},{... | collective-permute-start | bytes 786440 | tf_op jit(solution)/shard_map/ppermute | solution.py:26
  267.6 49.0 %collective-permute-start.4 = (bf16[128,1024]{1,0:T(8,128)(2,1)S(1)}, bf16[128,1024]{1,0:T(8,128)(2,1)S(1)}, u32[]{:S(2)}, u32[]{:S(2)}) collective-permute-start(bf16[128,1024]{1,0:T(8,128)(2,1)S(1)} %fusion.100), channel_id=1, source_target_pairs={{0,4},{1,5},{2,6},{3,7},{4,8},{5,9},{6,10},{7,11},{8,12},{9,13},{1... | collective-permute-start | bytes 786440 | tf_op jit(solution)/shard_map/ppermute | solution.py:26
  288.2 33.4 %collective-permute-start.5 = (bf16[128,1024]{1,0:T(8,128)(2,1)S(1)}, bf16[128,1024]{1,0:T(8,128)(2,1)S(1)}, u32[]{:S(2)}, u32[]{:S(2)}) collective-permute-start(bf16[128,1024]{1,0:T(8,128)(2,1)S(1)} %fusion.100), channel_id=1, source_target_pairs={{0,3},{1,4},{2,5},{3,6},{4,7},{5,8},{6,9},{7,10},{8,11},{9,12},{10... | collective-permute-start | bytes 786440 | tf_op jit(solution)/shard_map/ppermute | solution.py:26
  505.4 160.3 %copy-start = (f32[4,1152,128]{1,2,0:T(8,128)S(1)}, f32[4,1152,128]{1,2,0:T(8,128)}, u32[]{:S(2)}) copy-start(f32[4,1152,128]{1,2,0:T(8,128)} %get-tuple-element.61) | copy-start | bytes 7077892
  507.4 29.3 %collective-permute-start.8 = (f32[128,1024]{0,1:T(8,128)S(1)}, f32[128,1024]{0,1:T(8,128)S(1)}, u32[]{:S(2)}, u32[]{:S(2)}) collective-permute-start(f32[128,1024]{0,1:T(8,128)S(1)} %get-tuple-element.158), channel_id=1, source_target_pairs={{1,0},{2,1},{3,2},{4,3},{5,4},{6,5},{7,6},{8,7},{9,8},{10,9},{11,1... | collective-permute-start | bytes 1572872 | tf_op jit(solution)/shard_map/ppermute | solution.py:26
  521.7 19.4 %collective-permute-start.9 = (f32[128,1024]{0,1:T(8,128)S(1)}, f32[128,1024]{0,1:T(8,128)S(1)}, u32[]{:S(2)}, u32[]{:S(2)}) collective-permute-start(f32[128,1024]{0,1:T(8,128)S(1)} %get-tuple-element.159), channel_id=1, source_target_pairs={{2,0},{3,1},{4,2},{5,3},{6,4},{7,5},{8,6},{9,7},{10,8},{11,9},{12,... | collective-permute-start | bytes 1572872 | tf_op jit(solution)/shard_map/ppermute | solution.py:26
  526.4 38.0 %collective-permute-start.10 = (f32[128,1024]{0,1:T(8,128)S(1)}, f32[128,1024]{0,1:T(8,128)S(1)}, u32[]{:S(2)}, u32[]{:S(2)}) collective-permute-start(f32[128,1024]{0,1:T(8,128)S(1)} %get-tuple-element.160), channel_id=1, source_target_pairs={{3,0},{4,1},{5,2},{6,3},{7,4},{8,5},{9,6},{10,7},{11,8},{12,9},{13... | collective-permute-start | bytes 1572872 | tf_op jit(solution)/shard_map/ppermute | solution.py:26
  531.1 48.3 %collective-permute-start.11 = (f32[128,1024]{0,1:T(8,128)S(1)}, f32[128,1024]{0,1:T(8,128)S(1)}, u32[]{:S(2)}, u32[]{:S(2)}) collective-permute-start(f32[128,1024]{0,1:T(8,128)S(1)} %get-tuple-element.161), channel_id=1, source_target_pairs={{4,0},{5,1},{6,2},{7,3},{8,4},{9,5},{10,6},{11,7},{12,8},{13,9},{1... | collective-permute-start | bytes 1572872 | tf_op jit(solution)/shard_map/ppermute | solution.py:26
  534.7 61.3 %collective-permute-start.12 = (f32[128,1024]{0,1:T(8,128)S(1)}, f32[128,1024]{0,1:T(8,128)S(1)}, u32[]{:S(2)}, u32[]{:S(2)}) collective-permute-start(f32[128,1024]{0,1:T(8,128)S(1)} %get-tuple-element.162), channel_id=1, source_target_pairs={{5,0},{6,1},{7,2},{8,3},{9,4},{10,5},{11,6},{12,7},{13,8},{14,9},{... | collective-permute-start | bytes 1572872 | tf_op jit(solution)/shard_map/ppermute | solution.py:26
  536.6 117.9 %collective-permute-start.13 = (f32[128,1024]{0,1:T(8,128)S(1)}, f32[128,1024]{0,1:T(8,128)S(1)}, u32[]{:S(2)}, u32[]{:S(2)}) collective-permute-start(f32[128,1024]{0,1:T(8,128)S(1)} %get-tuple-element.163), channel_id=1, source_target_pairs={{6,0},{7,1},{8,2},{9,3},{10,4},{11,5},{12,6},{13,7},{14,8},{15,9},... | collective-permute-start | bytes 1572872 | tf_op jit(solution)/shard_map/ppermute | solution.py:26
  541.1 113.4 %collective-permute-start.15 = (f32[128,1024]{0,1:T(8,128)S(1)}, f32[128,1024]{0,1:T(8,128)S(1)}, u32[]{:S(2)}, u32[]{:S(2)}) collective-permute-start(f32[128,1024]{0,1:T(8,128)S(1)} %get-tuple-element.164), channel_id=1, source_target_pairs={{8,0},{9,1},{10,2},{11,3},{12,4},{13,5},{14,6},{15,7},{16,8},{17,9... | collective-permute-start | bytes 1572872 | tf_op jit(solution)/shard_map/ppermute | solution.py:26
  564.4 100.4 %copy-start.2 = (f32[128,1024]{0,1:T(8,128)}, f32[128,1024]{0,1:T(8,128)S(1)}, u32[]{:S(2)}) copy-start(f32[128,1024]{0,1:T(8,128)S(1)} %collective-permute-done.10) | copy-start | bytes 1572868
  564.4 100.4 %collective-permute-start.14 = (f32[128,1024]{0,1:T(8,128)S(1)}, f32[128,1024]{0,1:T(8,128)S(1)}, u32[]{:S(2)}, u32[]{:S(2)}) collective-permute-start(f32[128,1024]{0,1:T(8,128)S(1)} %get-tuple-element.165), channel_id=1, source_target_pairs={{7,0},{8,1},{9,2},{10,3},{11,4},{12,5},{13,6},{14,7},{15,8},{16,9}... | collective-permute-start | bytes 1572872 | tf_op jit(solution)/shard_map/ppermute | solution.py:26
  579.4 85.4 %copy-start.3 = (f32[128,1024]{0,1:T(8,128)}, f32[128,1024]{0,1:T(8,128)S(1)}, u32[]{:S(2)}) copy-start(f32[128,1024]{0,1:T(8,128)S(1)} %collective-permute-done.11) | copy-start | bytes 1572868
  666.6 382.3 %all-gather.12.cloned.1.call-start = ((), (), s32[]{:S(2)}) async-start(), calls=%async_computation.4 | async-start | bytes 35651584 | tf_op jit(solution)/shard_map/all_gather | solution.py:119
  (6 other events, 94.9 us)
Sparse Core Ops, SparseCore 0:
  10.4 41.9 all-gather.5
  54.2 173.7 all-gather.7
  666.8 174.2 all-gather.9
  847.7 201.1 all-gather.11
